TPU v7x, 512 devices: a whole 4x8x8 slice. The times are simulated.
512 devices in a mesh: fsdp: 64 (over y, x, core), cent: 8 (over z).
Axes of the slice: x: 4, y: 8, z: 8, core: 2. Of those that a mesh axis runs over, the one named last changes fastest.
Arguments:
- attention: bfloat16 [8192, 4096], P('fsdp', 'cent'), may hold values from -6 to 6
- w_out: bfloat16 [4096, 4096], P('cent', 'fsdp'), may hold values from -0.09375 to 0.09375
- hidden: bfloat16 [8192, 4096], P(('fsdp', 'cent')), may hold values from -6 to 6
- norm_gain: bfloat16 [4096], replicated, may hold values from 0.099609375 to 1.8984375
- centroids: bfloat16 [512, 4096], P('cent'), may hold values from -3 to 3
- token_codes: int32 [8192], P(('fsdp', 'cent')), may hold values from 0 to 63, as said below
- tile_lists: int32 [64, 8], P('fsdp'), may hold values from 0 to 63, as said below
Outputs:
- centroid_sums: float32 [512, 4096], P('cent', 'fsdp')
- residual_gram: float32 [4096, 4096], P('fsdp', 'cent')
Inputs may be any that keep to these rules, and one draw needn't show every extreme that they name: `token_codes`: token t belongs to block t // 128; its code k names centroid k % 8 of the tile at slot k // 8 of that block's list; every slot of a block's list is used. `tile_lists`: each row holds 8 distinct tile ids in ascending order; tile j holds centroids j * 8 to j * 8 + 7, and centroid g belongs to owner shard g // 64; in every row at most 2 listed tiles share an owner, and exactly 2 do for some owner.
All inputs are finite; a program needn't handle non-finite values.
Results may differ from a plain program's by a relative error of at most 0.0085.
Values may be sent and summed in bfloat16 or wider, within the bound.
A program may use at most 64 MiB of HBM per device.

v0:
```python
import jax
import jax.numpy as jnp
from jax import lax
from jax.sharding import PartitionSpec as P

TILE = 8
LT = 8


def shards(attention, w_out, hidden, norm_gain, centroids, token_codes, tile_lists):
    tok_dev = hidden.shape[0]
    feat_dim = hidden.shape[1]
    n_fsdp = lax.axis_size("fsdp")
    n_cent = lax.axis_size("cent")
    cap_slots = max(2, 2 * LT // n_cent)
    partial_out = jnp.dot(
        attention,
        lax.all_gather(w_out, "fsdp", axis=1, tiled=True),
        preferred_element_type=jnp.float32,
    )
    head_sum = lax.psum_scatter(
        partial_out.astype(jnp.bfloat16), "cent", scatter_dimension=0, tiled=True
    ).astype(jnp.float32)
    mixed_rows = hidden.astype(jnp.float32) + head_sum
    normed = (
        mixed_rows
        * lax.rsqrt(jnp.mean(mixed_rows * mixed_rows, axis=1, keepdims=True) + 1e-05)
        * norm_gain.astype(jnp.float32)
    )
    cent_dev = centroids.shape[0]
    own_tiles = cent_dev // TILE
    owner_idx = lax.axis_index("cent")
    listed = tile_lists[0]
    local_tile = listed - owner_idx * own_tiles
    owned_here = (local_tile >= 0) & (local_tile < own_tiles)
    safe_tile = jnp.clip(local_tile, 0, own_tiles - 1)
    tiles_here = centroids.reshape(own_tiles, TILE, feat_dim)
    slot_of = token_codes // TILE
    offset = token_codes % TILE
    rank_mine = jnp.cumsum(owned_here.astype(jnp.int32)) - 1
    chosen = owned_here[None, :] & (
        rank_mine[None, :] == jnp.arange(cap_slots, dtype=jnp.int32)[:, None]
    )
    send_tile = jnp.sum(jnp.where(chosen, safe_tile[None, :], 0), axis=1)
    filled = jnp.any(chosen, axis=1)
    outgoing = jnp.where(
        filled[:, None, None],
        jnp.take(tiles_here, send_tile, axis=0),
        jnp.zeros((cap_slots, TILE, feat_dim), jnp.bfloat16),
    )
    arrived = lax.all_gather(outgoing, "cent", axis=0, tiled=True)
    owner_of = listed // own_tiles
    list_pos = jnp.arange(LT, dtype=jnp.int32)
    earlier = (owner_of[None, :] == owner_of[:, None]) & (list_pos[None, :] < list_pos[:, None])
    rank_all = jnp.sum(earlier.astype(jnp.int32), axis=1)
    where_tile = owner_of * cap_slots + rank_all
    tile_rows = arrived.reshape(-1, feat_dim)
    centers = jnp.take(tile_rows, where_tile[slot_of] * TILE + offset, axis=0)
    residual = (normed - centers.astype(jnp.float32)).astype(jnp.bfloat16)
    onehot = (token_codes[None, :] == jnp.arange(LT * TILE, dtype=jnp.int32)[:, None]).astype(
        jnp.bfloat16
    )
    slot_part = jnp.dot(onehot, residual, preferred_element_type=jnp.float32)
    slot_sum = lax.psum(slot_part.astype(jnp.bfloat16), "cent").astype(jnp.float32)
    target = (local_tile[:, None] * TILE + jnp.arange(TILE, dtype=jnp.int32)[None, :]).reshape(-1)
    valid_rows = jnp.repeat(owned_here, TILE)
    placer = (
        (jnp.arange(cent_dev, dtype=jnp.int32)[:, None] == target[None, :]) & valid_rows[None, :]
    ).astype(jnp.float32)
    dense_part = jnp.dot(
        placer, slot_sum, precision=lax.Precision.HIGHEST, preferred_element_type=jnp.float32
    )
    centroid_sums = lax.psum_scatter(dense_part, "fsdp", scatter_dimension=1, tiled=True)
    rows_dev = feat_dim // n_fsdp
    row_start = lax.axis_index("fsdp") * rows_dev
    shard_rows = lax.all_gather(residual, "fsdp", axis=0, tiled=True)
    left_cols = lax.dynamic_slice_in_dim(shard_rows, row_start, rows_dev, 1)
    gram_part = lax.dot_general(
        left_cols, shard_rows, (((0,), (0,)), ((), ())), preferred_element_type=jnp.float32
    )
    gram_sum = lax.psum_scatter(gram_part, "cent", scatter_dimension=1, tiled=True)
    tokens_all = tok_dev * n_fsdp * n_cent
    return (centroid_sums, gram_sum / tokens_all)


def solution(mesh):
    in_specs = (
        P("fsdp", "cent"),
        P("cent", "fsdp"),
        P(("fsdp", "cent"), None),
        P(),
        P("cent", None),
        P(("fsdp", "cent")),
        P("fsdp", None),
    )
    out_specs = (P("cent", "fsdp"), P("fsdp", "cent"))
    return jax.shard_map(shards, mesh=mesh, in_specs=in_specs, out_specs=out_specs, check_vma=False)
```

profile of v0, /device:TPU:2, one launch (start us, length us, event | category | flops | bytes accessed | tf_op | source)
XLA Modules:
  0.0 561.0 jit_solution(6380447563696765636)
XLA Ops:
  7.2 0.0 copy-start
  7.2 0.0 copy-start.4
  7.2 0.0 copy-start.3
  7.2 0.0 copy-start.5
  7.2 0.0 all-gather.4.cloned.1.call-start
  7.3 0.7 all-gather.4.cloned.1.call-update
  7.9 0.0 all-gather.6.cloned.1.call-start
  8.0 0.7 convert_bitcast_fusion
  8.7 0.2 reduce-window.8
  8.9 0.7 fusion.11
  9.5 0.1 select_reduce_fusion
  9.7 0.0 copy-done
  9.7 0.6 gather_fusion.1
  10.2 0.1 fusion.8
  10.4 0.7 select_select_fusion
  11.1 0.0 copy-start.2
  11.1 0.0 all-gather.6.cloned.1.call-update
  11.1 0.0 reduce-scatter.6.cloned.1.call-start
  11.2 88.0 %all-gather.4.cloned.1.call-done = bf16[512,4096]{0,1:T(8,128)(2,1)} async-done(((bf16[512,64]{0,1:T(8,128)(2,1)}), bf16[512,4096]{0,1:T(8,128)(2,1)}) %all-gather.4.cloned.1.call-update) | async-done | bytes 4194320 | tf_op jit(solution)/shard_map/all_gather | solution.py:18
  99.2 4.8 convolution_convert_fusion
  104.0 0.0 reduce-scatter.6.cloned.1.call-update
  104.0 0.0 all-reduce.2.cloned.1.call-start
  104.1 0.0 copy-done.3
  104.1 0.0 copy-done.5
  104.1 0.0 copy-done.4
  104.1 0.2 convert_reduce_fusion
  104.3 0.7 gather_fusion
  105.0 37.3 %all-gather.6.cloned.1.call-done = bf16[16,8,4096]{2,1,0:T(8,128)(2,1)} async-done(((bf16[2,8,4096]{2,1,0:T(8,128)(2,1)}), bf16[16,8,4096]{2,1,0:T(8,128)(2,1)}) %all-gather.6.cloned.1.call-update) | async-done | bytes 1048592 | tf_op jit(solution)/shard_map/all_gather | solution.py:51
  142.4 2.1 gather_fusion.2
  144.5 41.3 %reduce-scatter.6.cloned.1.call-done = bf16[16,4096]{1,0:T(8,128)(2,1)} async-done(((bf16[128,4096]{1,0:T(8,128)(2,1)}), bf16[16,4096]{1,0:T(8,128)(2,1)}) %reduce-scatter.6.cloned.1.call-update) | async-done | bytes 131088 | tf_op jit(solution)/shard_map/reduce_scatter | solution.py:21
  185.8 0.0 copy-done.2
  185.8 1.1 multiply_reduce_fusion
  186.9 1.0 subtract_convert_fusion
  187.9 0.0 copy-start.1
  187.9 1.1 convolution_convert_fusion.1
  189.1 0.0 all-reduce.2.cloned.1.call-update
  189.1 0.0 all-gather.8.cloned.1.call-start
  189.1 0.0 copy-done.1
  189.1 0.5 all-gather.8.cloned.1.call-update
  189.7 0.0 reduce-scatter.10.cloned.1.call-start
  189.7 0.1 iota_add_fusion
  189.8 0.1 add.94
  189.9 0.1 broadcast_in_dim.69
  190.0 0.1 and.75
  190.1 77.2 %all-reduce.2.cloned.1.call-done = bf16[64,4096]{1,0:T(8,128)(2,1)} async-done(((bf16[64,4096]{1,0:T(8,128)(2,1)}), bf16[64,4096]{1,0:T(8,128)(2,1)}) %all-reduce.2.cloned.1.call-update) | async-done | bytes 524304 | tf_op jit(solution)/shard_map/psum | solution.py:64
  267.3 2.9 convolution_bitcast_fusion
  270.2 0.0 reduce-scatter.10.cloned.1.call-update
  270.2 0.0 reduce-scatter.8.cloned.1.call-start
  270.3 85.8 %all-gather.8.cloned.1.call-done = bf16[1024,4096]{1,0:T(8,128)(2,1)} async-done(((bf16[16,4096]{1,0:T(8,128)(2,1)}), bf16[1024,4096]{1,0:T(8,128)(2,1)}) %all-gather.8.cloned.1.call-update) | async-done | bytes 8388624 | tf_op jit(solution)/shard_map/all_gather | solution.py:76
  356.1 6.1 %fusion = f32[64,4096]{1,0:T(8,128)} fusion(bf16[1024,4096]{1,0:T(8,128)(2,1)} %all-gather.8.cloned.1.call-done, s32[]{:T(128)S(6)} %select_n.78), kind=kOutput, calls=%fused_computation.6 | convolution fusion | flops 536870912 | bytes 9699332 | tf_op jit(solution)/shard_map/dot_general | solution.py:78
  362.3 0.0 reduce-scatter.8.cloned.1.call-update
  362.3 145.4 %reduce-scatter.10.cloned.1.call-done = f32[64,64]{1,0:T(8,128)} async-done(((f32[4096,64]{1,0:T(8,128)}), f32[64,64]{1,0:T(8,128)}) %reduce-scatter.10.cloned.1.call-update) | async-done | bytes 16400
  507.7 1.5 copy.10
  509.1 43.5 %reduce-scatter.8.cloned.1.call-done = f32[64,512]{1,0:T(8,128)} async-done(((f32[64,4096]{1,0:T(8,128)}), f32[64,512]{1,0:T(8,128)}) %reduce-scatter.8.cloned.1.call-update) | async-done | bytes 131088 | tf_op jit(solution)/shard_map/reduce_scatter | solution.py:81
  552.6 1.6 broadcast_multiply_fusion
  (13 shorter events, 0.1 us)
Async XLA Ops:
  7.2 2.5 copy-start
  7.2 96.9 %copy-start.4 = (s32[1,8]{1,0:T(1,128)S(1)}, s32[1,8]{1,0:T(1,128)}, u32[]{:S(2)}) copy-start(s32[1,8]{1,0:T(1,128)} %param.13) | copy-start | bytes 100
  7.2 96.9 %copy-start.3 = (bf16[4096]{0:T(1024)(128)(2,1)S(1)}, bf16[4096]{0:T(1024)(128)(2,1)}, u32[]{:S(2)}) copy-start(bf16[4096]{0:T(1024)(128)(2,1)} %param.10) | copy-start | bytes 24580
  7.2 96.9 %copy-start.5 = (s32[16]{0:T(128)S(1)}, s32[16]{0:T(128)}, u32[]{:S(2)}) copy-start(s32[16]{0:T(128)} %param.12) | copy-start | bytes 196
  7.2 92.0 %all-gather.4.cloned.1.call-start = ((), (), s32[]{:S(2)}) async-start(), calls=%async_computation.3 | async-start | bytes 4259840 | tf_op jit(solution)/shard_map/all_gather | solution.py:18
  7.9 134.4 %all-gather.6.cloned.1.call-start = ((), (), s32[]{:S(2)}) async-start(), calls=%async_computation.5 | async-start | bytes 1179648 | tf_op jit(solution)/shard_map/all_gather | solution.py:51
  11.1 174.7 %copy-start.2 = (bf16[16,4096]{1,0:T(8,128)(2,1)S(1)}, bf16[16,4096]{1,0:T(8,128)(2,1)}, u32[]{:S(2)}) copy-start(bf16[16,4096]{1,0:T(8,128)(2,1)} %param.9) | copy-start | bytes 393220
  11.1 174.7 %reduce-scatter.6.cloned.1.call-start = ((), (), s32[]{:S(2)}) async-start(), calls=%async_computation.4 | async-start | bytes 1179648 | tf_op jit(solution)/shard_map/reduce_scatter | solution.py:21
  104.0 163.3 %all-reduce.2.cloned.1.call-start = ((), (), s32[]{:S(2)}) async-start(), calls=%async_computation.6 | async-start | bytes 1048576 | tf_op jit(solution)/shard_map/psum | solution.py:64
  187.9 1.2 copy-start.1
  189.1 167.0 %all-gather.8.cloned.1.call-start = ((), (), s32[]{:S(2)}) async-start(), calls=%async_computation.7 | async-start | bytes 8519680 | tf_op jit(solution)/shard_map/all_gather | solution.py:76
  189.7 318.0 %reduce-scatter.10.cloned.1.call-start = ((), (), s32[]{:S(2)}) async-start(), calls=%async_computation.9 | async-start | bytes 2129920
  270.2 282.3 %reduce-scatter.8.cloned.1.call-start = ((), (), s32[]{:S(2)}) async-start(), calls=%async_computation.8 | async-start | bytes 1179648 | tf_op jit(solution)/shard_map/reduce_scatter | solution.py:81
Sparse Core Ops, SparseCore 0:
  11.4 87.8 all-gather.3
  101.9 40.4 all-gather.5
  145.2 40.5 reduce-scatter.5
  189.2 78.0 all-reduce.1
  271.1 84.9 all-gather.7
  360.6 147.0 reduce-scatter.9
  510.5 42.0 reduce-scatter.7
where the time goes:
time: 561 us
  waiting for transfers between devices  520 us (93%)
  matrix products  15 us (3%)
  between operations  14.3 us (3%)
  other arithmetic  6.51 us (1%)
    unnamed x8, waiting for transfers between devices  147 us
    all_gather x1, waiting for transfers between devices, shards(): lax.all_gather(w_out, 'fsdp', axis=1, tiled=True)  88 us
    all_gather x1, waiting for transfers between devices, shards(): shard_rows = lax.all_gather(residual, 'fsdp', axis=0, tiled=True)  85.8 us
    psum x1, waiting for transfers between devices, shards(): lax.psum(slot_part.astype(jnp.bfloat16), 'cent').astype(jnp.float32)  77.2 us
    reduce_scatter x1, waiting for transfers between devices, shards(): lax.psum_scatter(gram_part, 'cent', scatter_dimension=1, tiled=True)  43.5 us
    reduce_scatter x1, waiting for transfers between devices, shards(): lax.psum_scatter(partial_out.astype(jnp.bfloat16), 'cent', scatter_dimens...  41.3 us
    all_gather x1, waiting for transfers between devices, shards(): arrived = lax.all_gather(outgoing, 'cent', axis=0, tiled=True)  37.3 us
  transfers between devices with their start and end apart: 7, of which 7 were waited for; matrix products, arithmetic and copies ran while one was open for 4% of the time, Pallas kernels for 0%

commit v1 on v0

--- a/solution.py
+++ b/solution.py
@@ -61,7 +61,9 @@
         jnp.bfloat16
     )
     slot_part = jnp.dot(onehot, residual, preferred_element_type=jnp.float32)
-    slot_sum = lax.psum(slot_part.astype(jnp.bfloat16), "cent").astype(jnp.float32)
+    slot_sum = jnp.sum(lax.all_gather(slot_part.astype(jnp.bfloat16), "cent"), axis=0).astype(
+        jnp.float32
+    )
     target = (local_tile[:, None] * TILE + jnp.arange(TILE, dtype=jnp.int32)[None, :]).reshape(-1)
     valid_rows = jnp.repeat(owned_here, TILE)
     placer = (

time: 561 us -> 540 us (0.963)
  waiting for transfers between devices: 520 us -> 496 us
    psum x1 -> x0, waiting for transfers between devices: 77.2 us -> none  [shards(): lax.psum(slot_part.astype(jnp.bfloat16), 'cent').astype(jnp.float32)]
    all_gather x0 -> x1, waiting for transfers between devices: none -> 55.5 us  [shards(): lax.all_gather(slot_part.astype(jnp.bfloat16), 'cent')]
where the time goes in v1:
time: 540 us; the launch traced here: 539 us
  waiting for transfers between devices  496 us (92%)
  between operations  14.3 us (3%)
  matrix products  13.9 us (3%)
  other arithmetic  9.45 us (2%)
    unnamed x8, waiting for transfers between devices  147 us
    all_gather x1, waiting for transfers between devices, shards(): lax.all_gather(w_out, 'fsdp', axis=1, tiled=True)  88 us
    all_gather x1, waiting for transfers between devices, shards(): shard_rows = lax.all_gather(residual, 'fsdp', axis=0, tiled=True)  84 us
    all_gather x1, waiting for transfers between devices, shards(): lax.all_gather(slot_part.astype(jnp.bfloat16), 'cent')  55.5 us
    reduce_scatter x1, waiting for transfers between devices, shards(): lax.psum_scatter(gram_part, 'cent', scatter_dimension=1, tiled=True)  43.5 us
    reduce_scatter x1, waiting for transfers between devices, shards(): lax.psum_scatter(partial_out.astype(jnp.bfloat16), 'cent', scatter_dimens...  41.3 us
    all_gather x1, waiting for transfers between devices, shards(): arrived = lax.all_gather(outgoing, 'cent', axis=0, tiled=True)  37.3 us
  transfers between devices with their start and end apart: 7, of which 7 were waited for; matrix products, arithmetic and copies ran while one was open for 4% of the time, Pallas kernels for 0%

profile of v1, /device:TPU:2, one launch (start us, length us, event | category | flops | bytes accessed | tf_op | source)
XLA Modules:
  0.0 539.3 jit_solution(13561744380637968905)
XLA Ops:
  7.2 0.0 copy-start
  7.2 0.0 copy-start.4
  7.2 0.0 copy-start.3
  7.2 0.0 copy-start.5
  7.2 0.0 all-gather.6.cloned.1.call-start
  7.3 0.7 all-gather.6.cloned.1.call-update
  7.9 0.0 all-gather.8.cloned.1.call-start
  8.0 0.7 convert_bitcast_fusion
  8.7 0.2 reduce-window.8
  8.9 0.7 fusion.11
  9.5 0.1 select_reduce_fusion
  9.7 0.0 copy-done
  9.7 0.6 gather_fusion.1
  10.2 0.1 fusion.8
  10.4 0.7 select_select_fusion
  11.1 0.0 copy-start.2
  11.1 0.0 all-gather.8.cloned.1.call-update
  11.1 0.0 reduce-scatter.6.cloned.1.call-start
  11.2 88.0 %all-gather.6.cloned.1.call-done = bf16[512,4096]{0,1:T(8,128)(2,1)} async-done(((bf16[512,64]{0,1:T(8,128)(2,1)}), bf16[512,4096]{0,1:T(8,128)(2,1)}) %all-gather.6.cloned.1.call-update) | async-done | bytes 4194320 | tf_op jit(solution)/shard_map/all_gather | solution.py:18
  99.2 4.8 convolution_convert_fusion
  104.0 0.0 reduce-scatter.6.cloned.1.call-update
  104.0 0.0 all-gather.12.cloned.1.call-start
  104.1 0.0 copy-done.3
  104.1 0.0 copy-done.5
  104.1 0.0 copy-done.4
  104.1 0.2 convert_reduce_fusion
  104.3 0.7 gather_fusion
  105.0 37.3 %all-gather.8.cloned.1.call-done = bf16[16,8,4096]{2,1,0:T(8,128)(2,1)} async-done(((bf16[2,8,4096]{2,1,0:T(8,128)(2,1)}), bf16[16,8,4096]{2,1,0:T(8,128)(2,1)}) %all-gather.8.cloned.1.call-update) | async-done | bytes 1048592 | tf_op jit(solution)/shard_map/all_gather | solution.py:51
  142.4 2.1 gather_fusion.2
  144.5 41.3 %reduce-scatter.6.cloned.1.call-done = bf16[16,4096]{1,0:T(8,128)(2,1)} async-done(((bf16[128,4096]{1,0:T(8,128)(2,1)}), bf16[16,4096]{1,0:T(8,128)(2,1)}) %reduce-scatter.6.cloned.1.call-update) | async-done | bytes 131088 | tf_op jit(solution)/shard_map/reduce_scatter | solution.py:21
  185.8 0.0 copy-done.2
  185.8 1.1 multiply_reduce_fusion
  186.9 1.0 subtract_convert_fusion
  187.9 0.0 copy-start.1
  187.9 1.1 convolution_convert_fusion.1
  189.0 0.0 all-gather.12.cloned.1.call-update
  189.0 0.0 all-gather.10.cloned.1.call-start
  189.1 0.0 copy-done.1
  189.1 0.5 all-gather.10.cloned.1.call-update
  189.6 0.0 reduce-scatter.10.cloned.1.call-start
  189.7 0.1 iota_add_fusion
  189.8 0.1 add.92
  189.8 0.1 broadcast_in_dim.69
  189.9 0.1 and.75
  190.0 55.5 %all-gather.12.cloned.1.call-done = bf16[512,4096]{1,0:T(8,128)(2,1)} async-done(((bf16[64,4096]{1,0:T(8,128)(2,1)}), bf16[512,4096]{1,0:T(8,128)(2,1)}) %all-gather.12.cloned.1.call-update) | async-done | bytes 4194320 | tf_op jit(solution)/shard_map/all_gather | solution.py:64
  245.5 2.9 reduce_sum.45
  248.5 1.9 convolution_bitcast_fusion
  250.4 0.0 reduce-scatter.10.cloned.1.call-update
  250.4 0.0 reduce-scatter.8.cloned.1.call-start
  250.4 84.0 %all-gather.10.cloned.1.call-done = bf16[1024,4096]{1,0:T(8,128)(2,1)} async-done(((bf16[16,4096]{1,0:T(8,128)(2,1)}), bf16[1024,4096]{1,0:T(8,128)(2,1)}) %all-gather.10.cloned.1.call-update) | async-done | bytes 8388624 | tf_op jit(solution)/shard_map/all_gather | solution.py:78
  334.4 6.1 %fusion = f32[64,4096]{1,0:T(8,128)} fusion(bf16[1024,4096]{1,0:T(8,128)(2,1)} %all-gather.10.cloned.1.call-done, s32[]{:T(128)S(6)} %select_n.78), kind=kOutput, calls=%fused_computation.6 | convolution fusion | flops 536870912 | bytes 9699332 | tf_op jit(solution)/shard_map/dot_general | solution.py:80
  340.5 0.0 reduce-scatter.8.cloned.1.call-update
  340.6 145.4 %reduce-scatter.10.cloned.1.call-done = f32[64,64]{1,0:T(8,128)} async-done(((f32[4096,64]{1,0:T(8,128)}), f32[64,64]{1,0:T(8,128)}) %reduce-scatter.10.cloned.1.call-update) | async-done | bytes 16400
  486.0 1.5 copy.10
  487.4 43.5 %reduce-scatter.8.cloned.1.call-done = f32[64,512]{1,0:T(8,128)} async-done(((f32[64,4096]{1,0:T(8,128)}), f32[64,512]{1,0:T(8,128)}) %reduce-scatter.8.cloned.1.call-update) | async-done | bytes 131088 | tf_op jit(solution)/shard_map/reduce_scatter | solution.py:83
  530.9 1.6 broadcast_multiply_fusion
  (13 shorter events, 0.1 us)
Async XLA Ops:
  7.2 2.5 copy-start
  7.2 96.9 %copy-start.4 = (s32[1,8]{1,0:T(1,128)S(1)}, s32[1,8]{1,0:T(1,128)}, u32[]{:S(2)}) copy-start(s32[1,8]{1,0:T(1,128)} %param.13) | copy-start | bytes 100
  7.2 96.9 %copy-start.3 = (bf16[4096]{0:T(1024)(128)(2,1)S(1)}, bf16[4096]{0:T(1024)(128)(2,1)}, u32[]{:S(2)}) copy-start(bf16[4096]{0:T(1024)(128)(2,1)} %param.10) | copy-start | bytes 24580
  7.2 96.9 %copy-start.5 = (s32[16]{0:T(128)S(1)}, s32[16]{0:T(128)}, u32[]{:S(2)}) copy-start(s32[16]{0:T(128)} %param.12) | copy-start | bytes 196
  7.2 92.0 %all-gather.6.cloned.1.call-start = ((), (), s32[]{:S(2)}) async-start(), calls=%async_computation.3 | async-start | bytes 4259840 | tf_op jit(solution)/shard_map/all_gather | solution.py:18
  7.9 134.4 %all-gather.8.cloned.1.call-start = ((), (), s32[]{:S(2)}) async-start(), calls=%async_computation.5 | async-start | bytes 1179648 | tf_op jit(solution)/shard_map/all_gather | solution.py:51
  11.1 174.7 %copy-start.2 = (bf16[16,4096]{1,0:T(8,128)(2,1)S(1)}, bf16[16,4096]{1,0:T(8,128)(2,1)}, u32[]{:S(2)}) copy-start(bf16[16,4096]{1,0:T(8,128)(2,1)} %param.9) | copy-start | bytes 393220
  11.1 174.7 %reduce-scatter.6.cloned.1.call-start = ((), (), s32[]{:S(2)}) async-start(), calls=%async_computation.4 | async-start | bytes 1179648 | tf_op jit(solution)/shard_map/reduce_scatter | solution.py:21
  104.0 141.5 %all-gather.12.cloned.1.call-start = ((), (), s32[]{:S(2)}) async-start(), calls=%async_computation.8 | async-start | bytes 4718592 | tf_op jit(solution)/shard_map/all_gather | solution.py:64
  187.9 1.2 copy-start.1
  189.0 145.4 %all-gather.10.cloned.1.call-start = ((), (), s32[]{:S(2)}) async-start(), calls=%async_computation.6 | async-start | bytes 8519680 | tf_op jit(solution)/shard_map/all_gather | solution.py:78
  189.6 296.3 %reduce-scatter.10.cloned.1.call-start = ((), (), s32[]{:S(2)}) async-start(), calls=%async_computation.9 | async-start | bytes 2129920
  250.4 280.5 %reduce-scatter.8.cloned.1.call-start = ((), (), s32[]{:S(2)}) async-start(), calls=%async_computation.7 | async-start | bytes 1179648 | tf_op jit(solution)/shard_map/reduce_scatter | solution.py:83
Sparse Core Ops, SparseCore 0:
  11.4 87.8 all-gather.5
  101.9 40.4 all-gather.7
  145.2 40.5 reduce-scatter.5
  189.2 56.3 all-gather.11
  249.3 85.0 all-gather.9
  338.9 147.0 reduce-scatter.9
  488.8 42.0 reduce-scatter.7
